TPU v7x, 256 devices: a whole 4x4x8 slice. The times are simulated.
256 devices in a mesh: areal: 64 (over x, y, z_hi, core), layer: 4 (over z_lo).
Axes of the slice: x: 4, y: 4, z: 8 (z_hi: 2, z_lo: 4; z = z_hi * 4 + z_lo), core: 2. Of those that a mesh axis runs over, the one named last changes fastest.
Arguments:
- pressure: float32 [8, 2048, 1024], P(None, 'areal', 'layer'), may hold values from 0.7 to 1.4
- composition: float32 [9, 8, 2048, 1024], P(None, None, 'areal', 'layer'), may hold values from 0.02 to 1
- mass_old: float32 [9, 8, 2048, 1024], P(None, None, 'areal', 'layer'), may hold values from 0 to 0.3
- pore_volume: float32 [8, 2048, 1024], P(None, 'areal', 'layer'), may hold values from 0.5 to 2
- trans_x: float32 [8, 2048, 1024], P(None, 'areal', 'layer'), may hold values from 0.3 to 3
- trans_y: float32 [8, 2048, 1024], P(None, 'areal', 'layer'), may hold values from 0.3 to 3
- trans_z: float32 [8, 2048, 1024], P(None, 'areal', 'layer'), may hold values from 0.3 to 3
- volatility: float32 [9], replicated, may hold values from 1.5 to 3
- pressure_slope: float32 [9], replicated, may hold values from 0.2 to 1
- mixing: float32 [9, 9], replicated, may hold values from -3.5 to 3.5
- two_phase: int32 [4, 512], P(None, 'areal'), may hold values from 0 to 1, as said below
Outputs:
- residual: float32 [9, 8, 2048, 1024], P(None, None, 'areal', 'layer')
- new_pressure: float32 [8, 2048, 1024], P(None, 'areal', 'layer')
Inputs may be any that keep to these rules, and one draw needn't show every extreme that they name: `two_phase`: for each areal index, the 4 rows together flag exactly 16 of their bricks of that areal index, and one of the rows flags all of its 8 bricks of that areal index.
All inputs are finite; a program needn't handle non-finite values.
Results may differ from a plain program's by a relative error of at most 0.0003.
Values sent between devices are 32-bit elements; how exact they have to be, the bound alone decides.
A program may use at most 128 MiB of HBM per device.

v0:
```python
import functools

import jax
import jax.numpy as jnp
from jax import lax
from jax.experimental import pallas as pl
from jax.experimental.pallas import tpu as pltpu
from jax.sharding import PartitionSpec as P

SS_ITERS = 3
RR_ITERS = 3
light_count = 4
compress = 0.2
F32 = jnp.float32
BF16 = jnp.bfloat16
MESH = pl.DeviceIdType.MESH
TILE = 8
FIELDS = 12
YROWS = 16
VMEM_BYTES = 24 << 20


def total_of(values):
    return functools.reduce(lambda a, b: a + b, values)


def split_matrix(mix, comps):
    size = comps * TILE
    rows = lax.broadcasted_iota(jnp.int32, (size, comps), 0) // TILE
    cols = lax.broadcasted_iota(jnp.int32, (size, comps), 1)
    pick = (rows == cols).astype(F32)
    wide = lax.dot_general(
        jnp.dot(pick, mix, precision=lax.Precision.HIGHEST, preferred_element_type=F32),
        pick,
        (((1,), (1,)), ((), ())),
        precision=lax.Precision.HIGHEST,
        preferred_element_type=F32,
    )
    a = lax.broadcasted_iota(jnp.int32, (size, size), 0) % TILE
    b = lax.broadcasted_iota(jnp.int32, (size, size), 1) % TILE
    full = jnp.where(a == b, 2.0 * wide, 0.0)
    high = full.astype(BF16)
    return high, (full - high.astype(F32)).astype(BF16)


def mixed(w_ref, parts):
    stack = jnp.concatenate(parts, axis=0)
    high = stack.astype(BF16)
    low = (stack - high.astype(F32)).astype(BF16)
    out = (
        jnp.dot(w_ref[0], high, preferred_element_type=F32)
        + jnp.dot(w_ref[1], high, preferred_element_type=F32)
        + jnp.dot(w_ref[0], low, preferred_element_type=F32)
    )
    return [out[i * TILE : (i + 1) * TILE] for i in range(len(parts))]


def flash(feed, log_p, half_vol, half_slope, w_ref):
    comps = len(feed)
    base = [half_vol[i] - half_slope[i] * log_p for i in range(comps)]
    half_log = base
    moved = None
    for outer in range(SS_ITERS):
        if outer:
            pulled = mixed(w_ref, moved)
            half_log = [base[i] - 0.5 * jnp.tanh(pulled[i]) for i in range(comps)]
        q = [jnp.tanh(v) for v in half_log]
        h = [1.0 / v for v in q]
        centre = None
        for inner in range(RR_ITERS):
            if inner:
                q = [1.0 / (h[i] + centre) for i in range(comps)]
            fq = [feed[i] * q[i] for i in range(comps)]
            step = total_of(fq) / total_of([fq[i] * q[i] for i in range(comps)])
            centre = jnp.clip(step if centre is None else centre + step, -1.0, 1.0)
        moved = [feed[i] * (1.0 / (h[i] + centre)) for i in range(comps)]
    low = 1.0 - centre
    high = 1.0 + centre
    low = 0.25 * (low * low)
    high = high * high
    outer_sum, outer_diff = low + high, high - low
    return [moved[i] * (outer_sum * h[i] + outer_diff) for i in range(comps)]


def flash_kernel(
    comps,
    p_hbm, comp_hbm, mass_hbm, pv_hbm, tx_hbm, ty_hbm, tz_hbm, vol_hbm, slope_hbm, mix_hbm, two_hbm,
    comp, mass, mob, pvi, grads, xmob, ymob, newp,
    p, pv, tx, ty, tz, w_ref, mix, vol, slope, two, flags,
    msum, fsum, first, rest, rdiag, coup, mxh, myh,
    xsend, xrecv, ysend, yrecv, fxsend, fxrecv, fysend, fyrecv,
    in_sem, send_sem, recv_sem, send2_sem, recv2_sem,
):
    depth, width, span = p.shape
    here_a = lax.axis_index("areal")
    here_l = lax.axis_index("layer")
    na = lax.axis_size("areal")
    nl = lax.axis_size("layer")
    xm = (lax.rem(here_a + na - 1, na), here_l)
    xp = (lax.rem(here_a + 1, na), here_l)
    ym = (here_a, lax.rem(here_l + nl - 1, nl))
    yp = (here_a, lax.rem(here_l + 1, nl))

    loads = [
        pltpu.make_async_copy(src, dst, in_sem.at[i])
        for i, (src, dst) in enumerate(
            [
                (mix_hbm, mix), (vol_hbm, vol), (slope_hbm, slope), (two_hbm, two),
                (comp_hbm, comp), (p_hbm, p), (tx_hbm, tx), (ty_hbm, ty),
                (mass_hbm, mass), (pv_hbm, pv), (tz_hbm, tz),
            ]
        )
    ]
    for load in loads:
        load.start()
    barrier = pltpu.get_barrier_semaphore()
    for device in (xm, xp, ym, yp):
        pl.semaphore_signal(barrier, inc=1, device_id=device, device_id_type=MESH)
    for load in loads[:4]:
        load.wait()
    w_ref[0], w_ref[1] = split_matrix(mix[...], comps)
    half_vol = [(0.5 if i < light_count else -0.5) * vol[i] for i in range(comps)]
    half_slope = [0.5 * slope[i] for i in range(comps)]
    bricks = two.shape[1]
    brick_of = lax.broadcasted_iota(jnp.int32, (width, span), 0) // (width // bricks)
    flag = jnp.zeros((width, span), F32)
    for b in range(bricks):
        flag = jnp.where(brick_of == b, two[here_l, b].astype(F32), flag)
    flags[...] = flag
    for load in loads[4:8]:
        load.wait()

    lane = lax.broadcasted_iota(jnp.int32, (width, 128), 1)

    def pack(z, carry):
        packed = jnp.zeros((width, 128), F32)
        for side, cut in ((0, 0), (1, span - 128)):
            source = 0 if side == 0 else 127
            for k in range(FIELDS):
                if k < comps:
                    value = comp[k, z, :, cut : cut + 128]
                elif k == comps:
                    value = p[z, :, cut : cut + 128]
                elif k == comps + 1:
                    value = ty[z, :, cut : cut + 128]
                else:
                    value = flags[:, cut : cut + 128]
                target = side * YROWS + k
                moved = pltpu.roll(value, (target - source) % 128, 1)
                packed = jnp.where(lane == target, moved, packed)
        ymob[pl.ds(pl.multiple_of(z * width, width), width), :] = packed
        for side, row in ((0, 0), (1, width - 1)):
            for k in range(comps):
                xsend[side, k, pl.ds(z, 1), :] = comp[k, z, row : row + 1, :]
            xsend[side, comps, pl.ds(z, 1), :] = p[z, row : row + 1, :]
            xsend[side, comps + 1, pl.ds(z, 1), :] = tx[z, row : row + 1, :]
            xsend[side, comps + 2, pl.ds(z, 1), :] = flags[row : row + 1, :]
        return carry

    lax.fori_loop(0, depth, pack, 0)
    turned = jnp.transpose(ymob[...])
    ysend[0] = turned[:YROWS]
    ysend[1] = turned[YROWS : 2 * YROWS]
    pl.semaphore_wait(barrier, 4)
    sends = [
        pltpu.make_async_remote_copy(
            src_ref=src, dst_ref=dst, send_sem=send_sem.at[i], recv_sem=recv_sem.at[i],
            device_id=device, device_id_type=MESH,
        )
        for i, (src, dst, device) in enumerate(
            [
                (xsend.at[0], xrecv.at[1], xm), (xsend.at[1], xrecv.at[0], xp),
                (ysend.at[0], yrecv.at[1], ym), (ysend.at[1], yrecv.at[0], yp),
            ]
        )
    ]
    for send in sends:
        send.start()

    def cells(values, pressure, flagged):
        total = total_of(values)
        inverse = 1.0 / total
        feed = [v * inverse for v in values]
        moved = flash(feed, jnp.log(pressure), half_vol, half_slope, w_ref)
        return inverse, total * inverse, [
            jnp.where(flagged > 0.0, moved[i], feed[i]) for i in range(comps)
        ]

    blocks = width // TILE

    def block(step, carry):
        z = step // blocks
        rows = pl.ds(pl.multiple_of((step % blocks) * TILE, TILE), TILE)
        values = [comp[i, z, rows, :] for i in range(comps)]
        inverse, whole, found = cells(values, p[z, rows, :], flags[rows, :])
        pvi[z, rows, :] = inverse
        fsum[z, rows, :] = whole
        for i in range(comps):
            mob[i, z, rows, :] = found[i]
        msum[z, rows, :] = total_of(found)
        return carry

    lax.fori_loop(0, depth * blocks, block, 0, unroll=8)

    for load in loads[8:]:
        load.wait()
    for send in sends:
        send.wait()

    for side in range(2):
        values = [xrecv[side, k] for k in range(comps)]
        _, _, found = cells(values, xrecv[side, comps], xrecv[side, comps + 2])
        for i in range(comps):
            xmob[side, i] = found[i]
        mxh[side] = total_of(found)
    sub = lax.broadcasted_iota(jnp.int32, (TILE, span), 0)

    def both(k):
        return jnp.where(sub == 0, yrecv[0, k : k + 1, :], yrecv[1, k : k + 1, :])

    _, _, found = cells([both(k) for k in range(comps)], both(comps), both(comps + 2))
    together = found + [total_of(found), both(comps), both(comps + 1)]
    for side in range(2):
        for k, value in enumerate(together):
            myh[side * YROWS + k : side * YROWS + k + 1, :] = value[side : side + 1, :]
    ymob[...] = jnp.transpose(myh[...])

    row_id = lax.broadcasted_iota(jnp.int32, (width, span), 0)
    lane_id = lax.broadcasted_iota(jnp.int32, (width, span), 1)
    has_xm = (here_a > 0).astype(F32)
    has_xp = (here_a < na - 1).astype(F32)
    has_ym = (here_l > 0).astype(F32)
    has_yp = (here_l < nl - 1).astype(F32)

    def before_x(value, edge):
        return jnp.where(row_id == 0, edge, pltpu.roll(value, 1, 0))

    def after_x(value, edge):
        return jnp.where(row_id == width - 1, edge, pltpu.roll(value, width - 1, 0))

    def before_y(value, edge):
        return jnp.where(lane_id == 0, edge, pltpu.roll(value, 1, 1))

    def after_y(value, edge):
        return jnp.where(lane_id == span - 1, edge, pltpu.roll(value, span - 1, 1))

    def faces(z, carry):
        up = jnp.minimum(z + 1, depth - 1)
        down = jnp.maximum(z - 1, 0)
        zrow = pl.ds(z, 1)
        yrow = pl.ds(pl.multiple_of(z * width, width), width)
        here_p, here_m = p[z], msum[z]
        edge = ymob[yrow, :]
        em = [edge[:, k : k + 1] for k in (comps, comps + 1, comps + 2)]
        ep = [edge[:, YROWS + k : YROWS + k + 1] for k in (comps, comps + 1)]
        t_x, t_y = tx[z], ty[z]
        strength = [
            tz[z] * (z < depth - 1).astype(F32),
            tz[down] * (z > 0).astype(F32),
            jnp.where(row_id == width - 1, has_xp * t_x, t_x),
            before_x(t_x, has_xm * xrecv[0, comps + 1, zrow, :]),
            jnp.where(lane_id == span - 1, has_yp * t_y, t_y),
            before_y(t_y, has_ym * em[2]),
        ]
        near_p = [
            p[up], p[down],
            after_x(here_p, xrecv[1, comps, zrow, :]), before_x(here_p, xrecv[0, comps, zrow, :]),
            after_y(here_p, ep[1]), before_y(here_p, em[1]),
        ]
        near_m = [
            msum[up], msum[down],
            after_x(here_m, mxh[1, zrow, :]), before_x(here_m, mxh[0, zrow, :]),
            after_y(here_m, ep[0]), before_y(here_m, em[0]),
        ]
        volume = pv[z]
        balance = volume * fsum[z] - total_of([mass[i, z] for i in range(comps)])
        diagonal = compress * volume
        centre = None
        for f in range(6):
            twice = 2.0 * strength[f]
            fall = here_p - near_p[f]
            link = twice * (here_m + near_m[f])
            slope_f = twice * fall
            balance = balance + link * fall
            diagonal = diagonal + link
            grads[f, z] = slope_f
            coup[f, z] = link
            centre = slope_f if centre is None else centre + slope_f
        grads[6, z] = centre
        inverse = 1.0 / diagonal
        update = -balance * inverse
        first[z] = update
        rest[z] = -balance
        rdiag[z] = inverse
        pvi[z] = volume * pvi[z]
        fxsend[0, zrow, :] = update[0:1, :]
        fxsend[1, zrow, :] = update[width - 1 : width, :]
        left = update[:, 0:128]
        right = pltpu.roll(update[:, span - 128 : span], 2, 1)
        coup[6, z, :, 0:128] = jnp.where(lane == 0, left, right)
        return carry

    lax.fori_loop(0, depth, faces, 0)
    stacked = coup[6, :, :, 0:128].reshape(depth * width, 128)
    fysend[...] = jnp.transpose(stacked)[:TILE]
    sends = [
        pltpu.make_async_remote_copy(
            src_ref=src, dst_ref=dst, send_sem=send2_sem.at[i], recv_sem=recv2_sem.at[i],
            device_id=device, device_id_type=MESH,
        )
        for i, (src, dst, device) in enumerate(
            [
                (fxsend.at[0], fxrecv.at[1], xm), (fxsend.at[1], fxrecv.at[0], xp),
                (fysend, fyrecv.at[1], ym), (fysend, fyrecv.at[0], yp),
            ]
        )
    ]
    for send in sends:
        send.start()
    for send in sends:
        send.wait()
    myh[0:1, :] = fyrecv[0, 1:2, :]
    myh[1:2, :] = fyrecv[1, 0:1, :]
    coup[6, :, :, 0:128] = jnp.transpose(myh[...]).reshape(depth, width, 128)

    def update(z, carry):
        up = jnp.minimum(z + 1, depth - 1)
        down = jnp.maximum(z - 1, 0)
        zrow = pl.ds(z, 1)
        value = first[z]
        edge = coup[6, z, :, 0:128]
        near = [
            first[up], first[down],
            after_x(value, fxrecv[1, zrow, :]), before_x(value, fxrecv[0, zrow, :]),
            after_y(value, edge[:, 1:2]), before_y(value, edge[:, 0:1]),
        ]
        gathered = rest[z]
        for f in range(6):
            gathered = gathered + coup[f, z] * near[f]
        newp[z] = p[z] + gathered * rdiag[z]
        return carry

    lax.fori_loop(0, depth, update, 0)


def residual_kernel(
    comps, comp, mass, mob, pvi, grads, xmob, ymob, newp, out_hbm, newp_hbm, out, sem
):
    depth, width, span = pvi.shape
    row_id = lax.broadcasted_iota(jnp.int32, (width, span), 0)
    lane_id = lax.broadcasted_iota(jnp.int32, (width, span), 1)

    def level(z, i):
        up = jnp.minimum(z + 1, depth - 1)
        down = jnp.maximum(z - 1, 0)
        zrow = pl.ds(z, 1)
        here = mob[i, z]
        edge = ymob[pl.ds(pl.multiple_of(z * width, width), width), :]
        near = [
            mob[i, up],
            mob[i, down],
            jnp.where(row_id == width - 1, xmob[1, i, zrow, :], pltpu.roll(here, width - 1, 0)),
            jnp.where(row_id == 0, xmob[0, i, zrow, :], pltpu.roll(here, 1, 0)),
            jnp.where(
                lane_id == span - 1,
                edge[:, YROWS + i : YROWS + i + 1],
                pltpu.roll(here, span - 1, 1),
            ),
            jnp.where(lane_id == 0, edge[:, i : i + 1], pltpu.roll(here, 1, 1)),
        ]
        value = pvi[z] * comp[i, z] - mass[i, z] + grads[6, z] * here
        for f in range(6):
            value = value + grads[f, z] * near[f]
        out[i, z] = value

    copies = [pltpu.make_async_copy(newp, newp_hbm, sem.at[comps])]
    copies[0].start()
    for i in range(comps):

        def body(z, carry, i=i):
            level(z, i)
            return carry

        lax.fori_loop(0, depth, body, 0)
        copy = pltpu.make_async_copy(out.at[i], out_hbm.at[i], sem.at[i])
        copy.start()
        copies.append(copy)
    for copy in copies:
        copy.wait()


def on_device(
    pressure, composition, mass_old, pore_volume, trans_x, trans_y, trans_z,
    volatility, pressure_slope, mixing, two_phase,
):
    comps = composition.shape[0]
    grid = pressure.shape
    depth, width, span = grid
    big = (comps,) + grid
    anywhere = pl.BlockSpec(memory_space=pltpu.HBM)
    local = pl.BlockSpec(memory_space=pltpu.VMEM)
    dma = pltpu.SemaphoreType.DMA

    def array(shape):
        return jax.ShapeDtypeStruct(shape, F32)

    def scratch(shape):
        return pltpu.VMEM(shape, F32)

    comp, mass, mob, pvi, grads, xmob, ymob, newp = pl.pallas_call(
        functools.partial(flash_kernel, comps),
        name="flash",
        out_shape=(
            array(big), array(big), array(big), array(grid), array((7,) + grid),
            array((2, comps, depth, span)), array((depth * width, 128)), array(grid),
        ),
        in_specs=[anywhere] * 11,
        out_specs=(local,) * 8,
        scratch_shapes=[
            scratch(grid), scratch(grid), scratch(grid), scratch(grid), scratch(grid),
            pltpu.VMEM((2, comps * TILE, comps * TILE), BF16),
            scratch((comps, comps)),
            pltpu.SMEM((comps,), F32), pltpu.SMEM((comps,), F32),
            pltpu.SMEM(two_phase.shape, jnp.int32),
            scratch((width, span)),
            scratch(grid), scratch(grid), scratch(grid), scratch(grid), scratch(grid),
            scratch((7,) + grid),
            scratch((2, depth, span)), scratch((128, depth * width)),
            scratch((2, FIELDS, depth, span)), scratch((2, FIELDS, depth, span)),
            scratch((2, YROWS, depth * width)), scratch((2, YROWS, depth * width)),
            scratch((2, depth, span)), scratch((2, depth, span)),
            scratch((TILE, depth * width)), scratch((2, TILE, depth * width)),
            dma((11,)), dma((4,)), dma((4,)), dma((4,)), dma((4,)),
        ],
        compiler_params=pltpu.CompilerParams(
            collective_id=0, has_side_effects=True, vmem_limit_bytes=VMEM_BYTES
        ),
    )(
        *(
            pltpu.with_memory_space_constraint(value, pltpu.HBM)
            for value in (
                pressure, composition, mass_old, pore_volume, trans_x, trans_y, trans_z,
                volatility, pressure_slope, mixing, two_phase,
            )
        )
    )
    return pl.pallas_call(
        functools.partial(residual_kernel, comps),
        name="residual",
        out_shape=(array(big), array(grid)),
        in_specs=[local] * 8,
        out_specs=(anywhere, anywhere),
        scratch_shapes=[scratch(big), dma((comps + 1,))],
        compiler_params=pltpu.CompilerParams(vmem_limit_bytes=VMEM_BYTES),
    )(comp, mass, mob, pvi, grads, xmob, ymob, newp)


def solution(mesh):
    placed = (
        P(None, "areal", "layer"),
        P(None, None, "areal", "layer"),
        P(None, None, "areal", "layer"),
        P(None, "areal", "layer"),
        P(None, "areal", "layer"),
        P(None, "areal", "layer"),
        P(None, "areal", "layer"),
        P(),
        P(),
        P(),
        P(None, "areal"),
    )
    return jax.shard_map(
        on_device,
        mesh=mesh,
        in_specs=placed,
        out_specs=(P(None, None, "areal", "layer"), P(None, "areal", "layer")),
        check_vma=False,
    )
```

profile of v0, /device:TPU:32, one launch (start us, length us, event | category | flops | bytes accessed | tf_op | source)
XLA Modules:
  0.0 36.6 jit_solution(17493532185380339584)
XLA Ops:
  0.6 28.0 %flash.1 = (f32[9,8,32,256]{3,2,1,0:T(8,128)S(1)}, f32[9,8,32,256]{3,2,1,0:T(8,128)S(1)}, f32[9,8,32,256]{3,2,1,0:T(8,128)S(1)}, f32[8,32,256]{2,1,0:T(8,128)S(1...) custom-call(f32[8,32,256]{2,1,0:T(8,128)} %p_hbm.1, ...), custom_call_target="tpu_custom_call" | custom-call | tf_op jit(solution)/shard_map/flash/pallas_call | solution.py:410
  28.6 8.0 %residual.1 = (f32[9,8,32,256]{3,2,1,0:T(8,128)}, f32[8,32,256]{2,1,0:T(8,128)}) custom-call(f32[9,8,32,256]{3,2,1,0:T(8,128)S(1)} %get-tuple-element.10.comp, f32[9,8,32,256]{3,2,1,0:T(8,128)S(1)} %get-tuple-element.11.mass, f32[9,8,32,256]{3,2,1,0:T(8,128)S(1)} %get-tuple-element.12.mob, f32[8,32,256]{2,1,0:T(8,128)S(1)} %get-tuple-element.13.pvi, ...), custom_call_target="tpu_custom_call" | custom-call | tf_op jit(solution)/shard_map/residual/pallas_call | solution.py:447
where the time goes:
time: 36.7 us; the launch traced here: 36.6 us
  Pallas kernels  35.9 us (98%)
  between operations  0.64 us (2%)
    pallas_call x1, Pallas kernels, on_device(): pl.pallas_call(functools.partial(flash_kernel, comps), name='flash', out_...  28 us
    pallas_call x1, Pallas kernels, on_device(): pl.pallas_call(functools.partial(residual_kernel, comps), name='residual'...  7.97 us

commit v1 on v0

--- a/solution.py
+++ b/solution.py
@@ -85,8 +85,8 @@
 def flash_kernel(
     comps,
     p_hbm, comp_hbm, mass_hbm, pv_hbm, tx_hbm, ty_hbm, tz_hbm, vol_hbm, slope_hbm, mix_hbm, two_hbm,
-    comp, mass, mob, pvi, grads, xmob, ymob, newp,
-    p, pv, tx, ty, tz, w_ref, mix, vol, slope, two, flags,
+    out, newp,
+    comp, mass, mob, pvi, grads, xmob, ymob, p, pv, tx, ty, tz, w_ref, mix, vol, slope, two, flags,
     msum, fsum, first, rest, rdiag, coup, mxh, myh,
     xsend, xrecv, ysend, yrecv, fxsend, fxrecv, fysend, fyrecv,
     in_sem, send_sem, recv_sem, send2_sem, recv2_sem,
@@ -114,8 +114,22 @@
     for load in loads:
         load.start()
     barrier = pltpu.get_barrier_semaphore()
-    for device in (xm, xp, ym, yp):
-        pl.semaphore_signal(barrier, inc=1, device_id=device, device_id_type=MESH)
+    there = (here_a > 0, here_a < na - 1, here_l > 0, here_l < nl - 1)
+
+    def finish(sends):
+        when_there(send.wait_send for send in sends)
+        when_there(sends[i].wait_recv for i in (1, 0, 3, 2))
+
+    def when_there(actions):
+        for exists, action in zip(there, actions):
+            pl.when(exists)(action)
+
+    when_there(
+        functools.partial(
+            pl.semaphore_signal, barrier, inc=1, device_id=device, device_id_type=MESH
+        )
+        for device in (xm, xp, ym, yp)
+    )
     for load in loads[:4]:
         load.wait()
     w_ref[0], w_ref[1] = split_matrix(mix[...], comps)
@@ -157,11 +171,11 @@
             xsend[side, comps + 2, pl.ds(z, 1), :] = flags[row : row + 1, :]
         return carry
 
-    lax.fori_loop(0, depth, pack, 0)
+    lax.fori_loop(0, depth, pack, 0, unroll=4)
     turned = jnp.transpose(ymob[...])
     ysend[0] = turned[:YROWS]
     ysend[1] = turned[YROWS : 2 * YROWS]
-    pl.semaphore_wait(barrier, 4)
+    pl.semaphore_wait(barrier, total_of([exists.astype(jnp.int32) for exists in there]))
     sends = [
         pltpu.make_async_remote_copy(
             src_ref=src, dst_ref=dst, send_sem=send_sem.at[i], recv_sem=recv_sem.at[i],
@@ -174,8 +188,13 @@
             ]
         )
     ]
-    for send in sends:
-        send.start()
+    when_there(send.start for send in sends)
+
+    for exists, slot in zip(there, (xrecv.at[0], xrecv.at[1], yrecv.at[0], yrecv.at[1])):
+
+        @pl.when(jnp.logical_not(exists))
+        def _(slot=slot):
+            slot[...] = jnp.ones(slot.shape, F32)
 
     def cells(values, pressure, flagged):
         total = total_of(values)
@@ -204,8 +223,7 @@
 
     for load in loads[8:]:
         load.wait()
-    for send in sends:
-        send.wait()
+    finish(sends)
 
     for side in range(2):
         values = [xrecv[side, k] for k in range(comps)]
@@ -300,7 +318,7 @@
         coup[6, z, :, 0:128] = jnp.where(lane == 0, left, right)
         return carry
 
-    lax.fori_loop(0, depth, faces, 0)
+    lax.fori_loop(0, depth, faces, 0, unroll=2)
     stacked = coup[6, :, :, 0:128].reshape(depth * width, 128)
     fysend[...] = jnp.transpose(stacked)[:TILE]
     sends = [
@@ -315,10 +333,38 @@
             ]
         )
     ]
-    for send in sends:
-        send.start()
-    for send in sends:
-        send.wait()
+    when_there(send.start for send in sends)
+
+    def level(z, i):
+        up = jnp.minimum(z + 1, depth - 1)
+        down = jnp.maximum(z - 1, 0)
+        zrow = pl.ds(z, 1)
+        here = mob[i, z]
+        edge = ymob[pl.ds(pl.multiple_of(z * width, width), width), :]
+        near = [
+            mob[i, up], mob[i, down],
+            after_x(here, xmob[1, i, zrow, :]), before_x(here, xmob[0, i, zrow, :]),
+            after_y(here, edge[:, YROWS + i : YROWS + i + 1]), before_y(here, edge[:, i : i + 1]),
+        ]
+        value = pvi[z] * comp[i, z] - mass[i, z] + grads[6, z] * here
+        for f in range(6):
+            value = value + grads[f, z] * near[f]
+        out[i, z] = value
+
+    for i in range(comps):
+
+        def body(z, carry, i=i):
+            level(z, i)
+            return carry
+
+        lax.fori_loop(0, depth, body, 0, unroll=8)
+    finish(sends)
+    for exists, slot in zip(there, (fxrecv.at[0], fxrecv.at[1], fyrecv.at[0], fyrecv.at[1])):
+
+        @pl.when(jnp.logical_not(exists))
+        def _(slot=slot):
+            slot[...] = jnp.zeros(slot.shape, F32)
+
     myh[0:1, :] = fyrecv[0, 1:2, :]
     myh[1:2, :] = fyrecv[1, 0:1, :]
     coup[6, :, :, 0:128] = jnp.transpose(myh[...]).reshape(depth, width, 128)
@@ -340,51 +386,18 @@
         newp[z] = p[z] + gathered * rdiag[z]
         return carry
 
-    lax.fori_loop(0, depth, update, 0)
-
-
-def residual_kernel(
-    comps, comp, mass, mob, pvi, grads, xmob, ymob, newp, out_hbm, newp_hbm, out, sem
-):
-    depth, width, span = pvi.shape
-    row_id = lax.broadcasted_iota(jnp.int32, (width, span), 0)
-    lane_id = lax.broadcasted_iota(jnp.int32, (width, span), 1)
-
-    def level(z, i):
-        up = jnp.minimum(z + 1, depth - 1)
-        down = jnp.maximum(z - 1, 0)
-        zrow = pl.ds(z, 1)
-        here = mob[i, z]
-        edge = ymob[pl.ds(pl.multiple_of(z * width, width), width), :]
-        near = [
-            mob[i, up],
-            mob[i, down],
-            jnp.where(row_id == width - 1, xmob[1, i, zrow, :], pltpu.roll(here, width - 1, 0)),
-            jnp.where(row_id == 0, xmob[0, i, zrow, :], pltpu.roll(here, 1, 0)),
-            jnp.where(
-                lane_id == span - 1,
-                edge[:, YROWS + i : YROWS + i + 1],
-                pltpu.roll(here, span - 1, 1),
-            ),
-            jnp.where(lane_id == 0, edge[:, i : i + 1], pltpu.roll(here, 1, 1)),
-        ]
-        value = pvi[z] * comp[i, z] - mass[i, z] + grads[6, z] * here
-        for f in range(6):
-            value = value + grads[f, z] * near[f]
-        out[i, z] = value
-
-    copies = [pltpu.make_async_copy(newp, newp_hbm, sem.at[comps])]
-    copies[0].start()
-    for i in range(comps):
-
-        def body(z, carry, i=i):
-            level(z, i)
-            return carry
-
-        lax.fori_loop(0, depth, body, 0)
-        copy = pltpu.make_async_copy(out.at[i], out_hbm.at[i], sem.at[i])
+    lax.fori_loop(0, depth, update, 0, unroll=4)
+
+
+def write_kernel(value, newp, out_hbm, newp_hbm, sem):
+    copies = [
+        pltpu.make_async_copy(src, dst, sem.at[i])
+        for i, (src, dst) in enumerate(
+            [(value, out_hbm), (newp, newp_hbm)]
+        )
+    ]
+    for copy in copies:
         copy.start()
-        copies.append(copy)
     for copy in copies:
         copy.wait()
 
@@ -407,16 +420,15 @@
     def scratch(shape):
         return pltpu.VMEM(shape, F32)
 
-    comp, mass, mob, pvi, grads, xmob, ymob, newp = pl.pallas_call(
+    out, newp = pl.pallas_call(
         functools.partial(flash_kernel, comps),
         name="flash",
-        out_shape=(
-            array(big), array(big), array(big), array(grid), array((7,) + grid),
-            array((2, comps, depth, span)), array((depth * width, 128)), array(grid),
-        ),
+        out_shape=(array(big), array(grid)),
         in_specs=[anywhere] * 11,
-        out_specs=(local,) * 8,
+        out_specs=(local,) * 2,
         scratch_shapes=[
+            scratch(big), scratch(big), scratch(big), scratch(grid), scratch((7,) + grid),
+            scratch((2, comps, depth, span)), scratch((depth * width, 128)),
             scratch(grid), scratch(grid), scratch(grid), scratch(grid), scratch(grid),
             pltpu.VMEM((2, comps * TILE, comps * TILE), BF16),
             scratch((comps, comps)),
@@ -445,14 +457,14 @@
         )
     )
     return pl.pallas_call(
-        functools.partial(residual_kernel, comps),
-        name="residual",
+        write_kernel,
+        name="write",
         out_shape=(array(big), array(grid)),
-        in_specs=[local] * 8,
+        in_specs=[local] * 2,
         out_specs=(anywhere, anywhere),
-        scratch_shapes=[scratch(big), dma((comps + 1,))],
-        compiler_params=pltpu.CompilerParams(vmem_limit_bytes=VMEM_BYTES),
-    )(comp, mass, mob, pvi, grads, xmob, ymob, newp)
+        scratch_shapes=[dma((comps + 1,))],
+        compiler_params=pltpu.CompilerParams(vmem_limit_bytes=8 << 20),
+    )(out, newp)
 
 
 def solution(mesh):

time: 36.7 us -> 27.6 us (0.75)
  the two profiles are of different devices: /device:TPU:32 before, /device:TPU:6 now
where the time goes in v1:
time: 27.6 us; the launch traced here: 27.4 us
  Pallas kernels  26.8 us (97%)
  between operations  0.64 us (2%)
    pallas_call x1, Pallas kernels, on_device(): pl.pallas_call(functools.partial(flash_kernel, comps), name='flash', out_...  25.2 us
    pallas_call x1, Pallas kernels, on_device(): pl.pallas_call(write_kernel, name='write', out_shape=(array(big), array(g...  1.57 us

profile of v1, /device:TPU:6, one launch (start us, length us, event | category | flops | bytes accessed | tf_op | source)
XLA Modules:
  0.0 27.4 jit_solution(478511099086879265)
XLA Ops:
  0.6 25.2 %flash.1 = (f32[9,8,32,256]{3,2,1,0:T(8,128)S(1)}, f32[8,32,256]{2,1,0:T(8,128)S(1)}) custom-call(f32[8,32,256]{2,1,0:T(8,128)} %p_hbm.1, f32[9,8,32,256]{3,2,1,0:T(8,128)} %comp_hbm.1, f32[9,8,32,256]{3,2,1,0:T(8,128)} %mass_hbm.1, f32[8,32,256]{2,1,0:T(8,128)} %pv_hbm.1, f32[8,32,256]{2,1,0:T(8,128)} %tx_hbm.1, f32[8,32,256]{2,1,0:T(8,128)} %ty_hbm.1, ...), custom_call_target="tpu_custom_call" | custom-call | tf_op jit(solution)/shard_map/flash/pallas_call | solution.py:423
  25.8 1.6 %write.1 = (f32[9,8,32,256]{3,2,1,0:T(8,128)}, f32[8,32,256]{2,1,0:T(8,128)}) custom-call(f32[9,8,32,256]{3,2,1,0:T(8,128)S(1)} %get-tuple-element.4.value, f32[8,32,256]{2,1,0:T(8,128)S(1)} %get-tuple-element.5.newp), custom_call_target="tpu_custom_call" | custom-call | tf_op jit(solution)/shard_map/write/pallas_call | solution.py:459

commit v2 on v1

--- a/solution.py
+++ b/solution.py
@@ -17,6 +17,7 @@
 TILE = 8
 FIELDS = 12
 YROWS = 16
+UNROLL = 8
 VMEM_BYTES = 24 << 20
 
 
@@ -88,7 +89,7 @@
     out, newp,
     comp, mass, mob, pvi, grads, xmob, ymob, p, pv, tx, ty, tz, w_ref, mix, vol, slope, two, flags,
     msum, fsum, first, rest, rdiag, coup, mxh, myh,
-    xsend, xrecv, ysend, yrecv, fxsend, fxrecv, fysend, fyrecv,
+    xsend, xrecv, ysend, yrecv, fxsend, fxrecv, fxend, fysend, fyrecv,
     in_sem, send_sem, recv_sem, send2_sem, recv2_sem,
 ):
     depth, width, span = p.shape
@@ -116,13 +117,13 @@
     barrier = pltpu.get_barrier_semaphore()
     there = (here_a > 0, here_a < na - 1, here_l > 0, here_l < nl - 1)
 
-    def finish(sends):
-        when_there(send.wait_send for send in sends)
-        when_there(sends[i].wait_recv for i in (1, 0, 3, 2))
-
-    def when_there(actions):
-        for exists, action in zip(there, actions):
-            pl.when(exists)(action)
+    def when_there(actions, which=(0, 1, 2, 3)):
+        for i, action in zip(which, actions):
+            pl.when(there[i])(action)
+
+    def finish(sends, which):
+        when_there([sends[i].wait_send for i in which], which)
+        when_there([sends[i ^ 1].wait_recv for i in which], which)
 
     when_there(
         functools.partial(
@@ -175,7 +176,6 @@
     turned = jnp.transpose(ymob[...])
     ysend[0] = turned[:YROWS]
     ysend[1] = turned[YROWS : 2 * YROWS]
-    pl.semaphore_wait(barrier, total_of([exists.astype(jnp.int32) for exists in there]))
     sends = [
         pltpu.make_async_remote_copy(
             src_ref=src, dst_ref=dst, send_sem=send_sem.at[i], recv_sem=recv_sem.at[i],
@@ -188,7 +188,6 @@
             ]
         )
     ]
-    when_there(send.start for send in sends)
 
     for exists, slot in zip(there, (xrecv.at[0], xrecv.at[1], yrecv.at[0], yrecv.at[1])):
 
@@ -206,10 +205,14 @@
         ]
 
     blocks = width // TILE
-
-    def block(step, carry):
-        z = step // blocks
-        rows = pl.ds(pl.multiple_of((step % blocks) * TILE, TILE), TILE)
+    chunks = blocks * depth // UNROLL
+
+    def block(step):
+        inner = step // (2 * depth)
+        pair = step % (2 * depth)
+        z = pair // 2
+        place = (1 - inner) * (blocks - 1) * (pair % 2) + inner * (1 + pair % 2)
+        rows = pl.ds(pl.multiple_of(place * TILE, TILE), TILE)
         values = [comp[i, z, rows, :] for i in range(comps)]
         inverse, whole, found = cells(values, p[z, rows, :], flags[rows, :])
         pvi[z, rows, :] = inverse
@@ -217,50 +220,128 @@
         for i in range(comps):
             mob[i, z, rows, :] = found[i]
         msum[z, rows, :] = total_of(found)
-        return carry
-
-    lax.fori_loop(0, depth * blocks, block, 0, unroll=8)
-
+
+    def chunk(index, carry):
+        def body(step, inner):
+            block(index * UNROLL + step)
+            return inner
+
+        return lax.fori_loop(0, UNROLL, body, carry, unroll=True)
+
+    early = 1 - (here_a // 2) % 2
+    edge_chunks = chunks // 2
+    send_after = early * edge_chunks
+    share_after = edge_chunks + early * (chunks - edge_chunks)
+    lax.fori_loop(0, send_after, chunk, 0)
+    pl.semaphore_wait(barrier, total_of([exists.astype(jnp.int32) for exists in there]))
+    when_there(send.start for send in sends)
+    lax.fori_loop(send_after, share_after, chunk, 0)
     for load in loads[8:]:
         load.wait()
-    finish(sends)
-
+
+    finish(sends, (2, 3))
+    sub = lax.broadcasted_iota(jnp.int32, (TILE, span), 0)
+
+    def both(k):
+        return jnp.where(sub == 0, yrecv[0, k : k + 1, :], yrecv[1, k : k + 1, :])
+
+    _, _, found = cells([both(k) for k in range(comps)], both(comps), both(comps + 2))
+    together = found + [total_of(found), both(comps), both(comps + 1)]
+    for side in range(2):
+        for k, value in enumerate(together):
+            myh[side * YROWS + k : side * YROWS + k + 1, :] = value[side : side + 1, :]
+    ymob[...] = jnp.transpose(myh[...])
+
+    row_id = lax.broadcasted_iota(jnp.int32, (width, span), 0)
+    lane_id = lax.broadcasted_iota(jnp.int32, (width, span), 1)
+    has_xm = (here_a > 0).astype(F32)
+    has_xp = (here_a < na - 1).astype(F32)
+    has_ym = (here_l > 0).astype(F32)
+    has_yp = (here_l < nl - 1).astype(F32)
+
+    def before_x(value, edge):
+        return jnp.where(row_id == 0, edge, pltpu.roll(value, 1, 0))
+
+    def after_x(value, edge):
+        return jnp.where(row_id == width - 1, edge, pltpu.roll(value, width - 1, 0))
+
+    def before_y(value, edge):
+        return jnp.where(lane_id == 0, edge, pltpu.roll(value, 1, 1))
+
+    def after_y(value, edge):
+        return jnp.where(lane_id == span - 1, edge, pltpu.roll(value, span - 1, 1))
+
+    edge_lane = lax.broadcasted_iota(jnp.int32, (depth, span), 1)
+    level_id = lax.broadcasted_iota(jnp.int32, (depth, span), 0)
+
+    def row_of(ref, r):
+        return ref[:, r, :]
+
+    for side, row, inside in ((0, 0, 1), (1, width - 1, width - 2)):
+        edge = ymob[pl.ds(row, depth, stride=width), :]
+
+        def near_y(value, k, edge=edge):
+            return (
+                jnp.where(
+                    edge_lane == span - 1,
+                    edge[:, YROWS + k : YROWS + k + 1],
+                    pltpu.roll(value, span - 1, 1),
+                ),
+                jnp.where(edge_lane == 0, edge[:, k : k + 1], pltpu.roll(value, 1, 1)),
+            )
+
+        here_p, here_m = row_of(p, row), row_of(msum, row)
+        t_y, t_z = row_of(ty, row), row_of(tz, row)
+        strength = [
+            jnp.where(level_id == depth - 1, 0.0, t_z),
+            jnp.where(level_id == 0, 0.0, pltpu.roll(t_z, 1, 0)),
+            row_of(tx, min(row, inside)),
+            jnp.where(edge_lane == span - 1, has_yp * t_y, t_y),
+            jnp.where(
+                edge_lane == 0, has_ym * edge[:, comps + 2 : comps + 3], pltpu.roll(t_y, 1, 1)
+            ),
+        ]
+        near_p = [
+            pltpu.roll(here_p, depth - 1, 0), pltpu.roll(here_p, 1, 0), row_of(p, inside),
+            *near_y(here_p, comps + 1),
+        ]
+        near_m = [
+            pltpu.roll(here_m, depth - 1, 0), pltpu.roll(here_m, 1, 0), row_of(msum, inside),
+            *near_y(here_m, comps),
+        ]
+        volume = row_of(pv, row)
+        balance = volume * row_of(fsum, row) - total_of(
+            [mass[i, :, row, :] for i in range(comps)]
+        )
+        diagonal = compress * volume
+        for f in range(5):
+            link = 2.0 * strength[f] * (here_m + near_m[f])
+            balance = balance + link * (here_p - near_p[f])
+            diagonal = diagonal + link
+        fxsend[side, 0] = balance
+        fxsend[side, 1] = diagonal
+    shares = [
+        pltpu.make_async_remote_copy(
+            src_ref=src, dst_ref=dst, send_sem=send2_sem.at[i], recv_sem=recv2_sem.at[i],
+            device_id=device, device_id_type=MESH,
+        )
+        for i, (src, dst, device) in enumerate(
+            [
+                (fxsend.at[0], fxrecv.at[1], xm), (fxsend.at[1], fxrecv.at[0], xp),
+                (fysend, fyrecv.at[1], ym), (fysend, fyrecv.at[0], yp),
+            ]
+        )
+    ]
+    when_there([share.start for share in shares[:2]])
+    lax.fori_loop(share_after, chunks, chunk, 0)
+
+    finish(sends, (0, 1))
     for side in range(2):
         values = [xrecv[side, k] for k in range(comps)]
         _, _, found = cells(values, xrecv[side, comps], xrecv[side, comps + 2])
         for i in range(comps):
             xmob[side, i] = found[i]
         mxh[side] = total_of(found)
-    sub = lax.broadcasted_iota(jnp.int32, (TILE, span), 0)
-
-    def both(k):
-        return jnp.where(sub == 0, yrecv[0, k : k + 1, :], yrecv[1, k : k + 1, :])
-
-    _, _, found = cells([both(k) for k in range(comps)], both(comps), both(comps + 2))
-    together = found + [total_of(found), both(comps), both(comps + 1)]
-    for side in range(2):
-        for k, value in enumerate(together):
-            myh[side * YROWS + k : side * YROWS + k + 1, :] = value[side : side + 1, :]
-    ymob[...] = jnp.transpose(myh[...])
-
-    row_id = lax.broadcasted_iota(jnp.int32, (width, span), 0)
-    lane_id = lax.broadcasted_iota(jnp.int32, (width, span), 1)
-    has_xm = (here_a > 0).astype(F32)
-    has_xp = (here_a < na - 1).astype(F32)
-    has_ym = (here_l > 0).astype(F32)
-    has_yp = (here_l < nl - 1).astype(F32)
-
-    def before_x(value, edge):
-        return jnp.where(row_id == 0, edge, pltpu.roll(value, 1, 0))
-
-    def after_x(value, edge):
-        return jnp.where(row_id == width - 1, edge, pltpu.roll(value, width - 1, 0))
-
-    def before_y(value, edge):
-        return jnp.where(lane_id == 0, edge, pltpu.roll(value, 1, 1))
-
-    def after_y(value, edge):
-        return jnp.where(lane_id == span - 1, edge, pltpu.roll(value, span - 1, 1))
 
     def faces(z, carry):
         up = jnp.minimum(z + 1, depth - 1)
@@ -311,8 +392,6 @@
         rest[z] = -balance
         rdiag[z] = inverse
         pvi[z] = volume * pvi[z]
-        fxsend[0, zrow, :] = update[0:1, :]
-        fxsend[1, zrow, :] = update[width - 1 : width, :]
         left = update[:, 0:128]
         right = pltpu.roll(update[:, span - 128 : span], 2, 1)
         coup[6, z, :, 0:128] = jnp.where(lane == 0, left, right)
@@ -321,19 +400,7 @@
     lax.fori_loop(0, depth, faces, 0, unroll=2)
     stacked = coup[6, :, :, 0:128].reshape(depth * width, 128)
     fysend[...] = jnp.transpose(stacked)[:TILE]
-    sends = [
-        pltpu.make_async_remote_copy(
-            src_ref=src, dst_ref=dst, send_sem=send2_sem.at[i], recv_sem=recv2_sem.at[i],
-            device_id=device, device_id_type=MESH,
-        )
-        for i, (src, dst, device) in enumerate(
-            [
-                (fxsend.at[0], fxrecv.at[1], xm), (fxsend.at[1], fxrecv.at[0], xp),
-                (fysend, fyrecv.at[1], ym), (fysend, fyrecv.at[0], yp),
-            ]
-        )
-    ]
-    when_there(send.start for send in sends)
+    when_there([share.start for share in shares[2:]], (2, 3))
 
     def level(z, i):
         up = jnp.minimum(z + 1, depth - 1)
@@ -358,12 +425,18 @@
             return carry
 
         lax.fori_loop(0, depth, body, 0, unroll=8)
-    finish(sends)
+    finish(shares, (0, 1, 2, 3))
     for exists, slot in zip(there, (fxrecv.at[0], fxrecv.at[1], fyrecv.at[0], fyrecv.at[1])):
 
         @pl.when(jnp.logical_not(exists))
         def _(slot=slot):
-            slot[...] = jnp.zeros(slot.shape, F32)
+            slot[...] = jnp.ones(slot.shape, F32)
+
+    for side, row, exists in ((0, 0, has_xm), (1, width - 1, has_xp)):
+        face = xrecv[0, comps + 1] if side == 0 else row_of(tx, row)
+        link = 2.0 * exists * face * (mxh[side] + row_of(msum, row))
+        fall = xrecv[side, comps] - row_of(p, row)
+        fxend[side] = -(fxrecv[side, 0] + link * fall) / (fxrecv[side, 1] + link)
 
     myh[0:1, :] = fyrecv[0, 1:2, :]
     myh[1:2, :] = fyrecv[1, 0:1, :]
@@ -377,7 +450,7 @@
         edge = coup[6, z, :, 0:128]
         near = [
             first[up], first[down],
-            after_x(value, fxrecv[1, zrow, :]), before_x(value, fxrecv[0, zrow, :]),
+            after_x(value, fxend[1, zrow, :]), before_x(value, fxend[0, zrow, :]),
             after_y(value, edge[:, 1:2]), before_y(value, edge[:, 0:1]),
         ]
         gathered = rest[z]
@@ -440,7 +513,7 @@
             scratch((2, depth, span)), scratch((128, depth * width)),
             scratch((2, FIELDS, depth, span)), scratch((2, FIELDS, depth, span)),
             scratch((2, YROWS, depth * width)), scratch((2, YROWS, depth * width)),
-            scratch((2, depth, span)), scratch((2, depth, span)),
+            scratch((2, 2, depth, span)), scratch((2, 2, depth, span)), scratch((2, depth, span)),
             scratch((TILE, depth * width)), scratch((2, TILE, depth * width)),
             dma((11,)), dma((4,)), dma((4,)), dma((4,)), dma((4,)),
         ],

time: 27.6 us -> 25 us (0.906)
  Pallas kernels: 26.8 us -> 24.3 us
    pallas_call x1, Pallas kernels: 25.2 us -> 22.7 us  [on_device(): pl.pallas_call(functools.partial(flash_kernel, comps), name='flash', out_...]
where the time goes in v2:
time: 25 us; the launch traced here: 24.9 us
  Pallas kernels  24.3 us (97%)
  between operations  0.64 us (3%)
    pallas_call x1, Pallas kernels, on_device(): pl.pallas_call(functools.partial(flash_kernel, comps), name='flash', out_...  22.7 us
    pallas_call x1, Pallas kernels, on_device(): pl.pallas_call(write_kernel, name='write', out_shape=(array(big), array(g...  1.57 us

profile of v2, /device:TPU:6, one launch (start us, length us, event | category | flops | bytes accessed | tf_op | source)
XLA Modules:
  0.0 24.9 jit_solution(17564924237306340247)
XLA Ops:
  0.6 22.7 %flash.1 = (f32[9,8,32,256]{3,2,1,0:T(8,128)S(1)}, f32[8,32,256]{2,1,0:T(8,128)S(1)}) custom-call(f32[8,32,256]{2,1,0:T(8,128)} %p_hbm.1, f32[9,8,32,256]{3,2,1,0:T(8,128)} %comp_hbm.1, f32[9,8,32,256]{3,2,1,0:T(8,128)} %mass_hbm.1, f32[8,32,256]{2,1,0:T(8,128)} %pv_hbm.1, f32[8,32,256]{2,1,0:T(8,128)} %tx_hbm.1, f32[8,32,256]{2,1,0:T(8,128)} %ty_hbm.1, ...), custom_call_target="tpu_custom_call" | custom-call | tf_op jit(solution)/shard_map/flash/pallas_call | solution.py:496
  23.3 1.6 %write.1 = (f32[9,8,32,256]{3,2,1,0:T(8,128)}, f32[8,32,256]{2,1,0:T(8,128)}) custom-call(f32[9,8,32,256]{3,2,1,0:T(8,128)S(1)} %get-tuple-element.4.value, f32[8,32,256]{2,1,0:T(8,128)S(1)} %get-tuple-element.5.newp), custom_call_target="tpu_custom_call" | custom-call | tf_op jit(solution)/shard_map/write/pallas_call | solution.py:532

commit v3 on v2

--- a/solution.py
+++ b/solution.py
@@ -102,12 +102,18 @@
     ym = (here_a, lax.rem(here_l + nl - 1, nl))
     yp = (here_a, lax.rem(here_l + 1, nl))
 
+    low, high = pl.ds(0, TILE), pl.ds(width - TILE, TILE)
+    inner = pl.ds(TILE, width - 2 * TILE)
     loads = [
         pltpu.make_async_copy(src, dst, in_sem.at[i])
         for i, (src, dst) in enumerate(
             [
-                (mix_hbm, mix), (vol_hbm, vol), (slope_hbm, slope), (two_hbm, two),
-                (comp_hbm, comp), (p_hbm, p), (tx_hbm, tx), (ty_hbm, ty),
+                (two_hbm, two),
+                (comp_hbm.at[:, :, low, :], comp.at[:, :, low, :]),
+                (comp_hbm.at[:, :, high, :], comp.at[:, :, high, :]),
+                (p_hbm, p), (tx_hbm, tx),
+                (mix_hbm, mix), (vol_hbm, vol), (slope_hbm, slope),
+                (comp_hbm.at[:, :, inner, :], comp.at[:, :, inner, :]), (ty_hbm, ty),
                 (mass_hbm, mass), (pv_hbm, pv), (tz_hbm, tz),
             ]
         )
@@ -131,23 +137,98 @@
         )
         for device in (xm, xp, ym, yp)
     )
-    for load in loads[:4]:
+    for load in loads[:5]:
         load.wait()
-    w_ref[0], w_ref[1] = split_matrix(mix[...], comps)
-    half_vol = [(0.5 if i < light_count else -0.5) * vol[i] for i in range(comps)]
-    half_slope = [0.5 * slope[i] for i in range(comps)]
     bricks = two.shape[1]
     brick_of = lax.broadcasted_iota(jnp.int32, (width, span), 0) // (width // bricks)
     flag = jnp.zeros((width, span), F32)
     for b in range(bricks):
         flag = jnp.where(brick_of == b, two[here_l, b].astype(F32), flag)
     flags[...] = flag
-    for load in loads[4:8]:
+    def pack_x(z, carry):
+        for side, row in ((0, 0), (1, width - 1)):
+            for k in range(comps):
+                xsend[side, k, pl.ds(z, 1), :] = comp[k, z, row : row + 1, :]
+            xsend[side, comps, pl.ds(z, 1), :] = p[z, row : row + 1, :]
+            xsend[side, comps + 1, pl.ds(z, 1), :] = tx[z, row : row + 1, :]
+            xsend[side, comps + 2, pl.ds(z, 1), :] = flags[row : row + 1, :]
+        return carry
+
+    lax.fori_loop(0, depth, pack_x, 0, unroll=4)
+    lane = lax.broadcasted_iota(jnp.int32, (width, 128), 1)
+    sends = [
+        pltpu.make_async_remote_copy(
+            src_ref=src, dst_ref=dst, send_sem=send_sem.at[i], recv_sem=recv_sem.at[i],
+            device_id=device, device_id_type=MESH,
+        )
+        for i, (src, dst, device) in enumerate(
+            [
+                (xsend.at[0], xrecv.at[1], xm), (xsend.at[1], xrecv.at[0], xp),
+                (ysend.at[0], yrecv.at[1], ym), (ysend.at[1], yrecv.at[0], yp),
+            ]
+        )
+    ]
+
+    early = 1 - (here_a // 2) % 2
+
+    def send_x():
+        pl.semaphore_wait(barrier, total_of([exists.astype(jnp.int32) for exists in there]))
+        when_there([send.start for send in sends[:2]])
+
+    pl.when(early == 0)(send_x)
+    for load in loads[5:8]:
         load.wait()
-
-    lane = lax.broadcasted_iota(jnp.int32, (width, 128), 1)
-
-    def pack(z, carry):
+    w_ref[0], w_ref[1] = split_matrix(mix[...], comps)
+    half_vol = [(0.5 if i < light_count else -0.5) * vol[i] for i in range(comps)]
+    half_slope = [0.5 * slope[i] for i in range(comps)]
+    for exists, slot in zip(there, (xrecv.at[0], xrecv.at[1], yrecv.at[0], yrecv.at[1])):
+
+        @pl.when(jnp.logical_not(exists))
+        def _(slot=slot):
+            slot[...] = jnp.ones(slot.shape, F32)
+
+    def cells(values, pressure, flagged):
+        total = total_of(values)
+        inverse = 1.0 / total
+        feed = [v * inverse for v in values]
+        moved = flash(feed, jnp.log(pressure), half_vol, half_slope, w_ref)
+        return inverse, total * inverse, [
+            jnp.where(flagged > 0.0, moved[i], feed[i]) for i in range(comps)
+        ]
+
+    blocks = width // TILE
+    chunks = blocks * depth // UNROLL
+
+    def block(step):
+        inner = step // (2 * depth)
+        pair = step % (2 * depth)
+        z = pair // 2
+        place = (1 - inner) * (blocks - 1) * (pair % 2) + inner * (1 + pair % 2)
+        rows = pl.ds(pl.multiple_of(place * TILE, TILE), TILE)
+        values = [comp[i, z, rows, :] for i in range(comps)]
+        inverse, whole, found = cells(values, p[z, rows, :], flags[rows, :])
+        pvi[z, rows, :] = inverse
+        fsum[z, rows, :] = whole
+        for i in range(comps):
+            mob[i, z, rows, :] = found[i]
+        msum[z, rows, :] = total_of(found)
+
+    def chunk(index, carry):
+        def body(step, inner):
+            block(index * UNROLL + step)
+            return inner
+
+        return lax.fori_loop(0, UNROLL, body, carry, unroll=True)
+
+    edge_chunks = chunks // 2
+    send_after = early * edge_chunks
+    share_after = edge_chunks + early * (chunks - edge_chunks)
+    lax.fori_loop(0, send_after, chunk, 0)
+    pl.when(early == 1)(send_x)
+    for load in loads[8:10]:
+        load.wait()
+
+    def pack_y(z, carry):
         packed = jnp.zeros((width, 128), F32)
         for side, cut in ((0, 0), (1, span - 128)):
             source = 0 if side == 0 else 127
@@ -164,79 +245,15 @@
                 moved = pltpu.roll(value, (target - source) % 128, 1)
                 packed = jnp.where(lane == target, moved, packed)
         ymob[pl.ds(pl.multiple_of(z * width, width), width), :] = packed
-        for side, row in ((0, 0), (1, width - 1)):
-            for k in range(comps):
-                xsend[side, k, pl.ds(z, 1), :] = comp[k, z, row : row + 1, :]
-            xsend[side, comps, pl.ds(z, 1), :] = p[z, row : row + 1, :]
-            xsend[side, comps + 1, pl.ds(z, 1), :] = tx[z, row : row + 1, :]
-            xsend[side, comps + 2, pl.ds(z, 1), :] = flags[row : row + 1, :]
         return carry
 
-    lax.fori_loop(0, depth, pack, 0, unroll=4)
+    lax.fori_loop(0, depth, pack_y, 0, unroll=4)
     turned = jnp.transpose(ymob[...])
     ysend[0] = turned[:YROWS]
     ysend[1] = turned[YROWS : 2 * YROWS]
-    sends = [
-        pltpu.make_async_remote_copy(
-            src_ref=src, dst_ref=dst, send_sem=send_sem.at[i], recv_sem=recv_sem.at[i],
-            device_id=device, device_id_type=MESH,
-        )
-        for i, (src, dst, device) in enumerate(
-            [
-                (xsend.at[0], xrecv.at[1], xm), (xsend.at[1], xrecv.at[0], xp),
-                (ysend.at[0], yrecv.at[1], ym), (ysend.at[1], yrecv.at[0], yp),
-            ]
-        )
-    ]
-
-    for exists, slot in zip(there, (xrecv.at[0], xrecv.at[1], yrecv.at[0], yrecv.at[1])):
-
-        @pl.when(jnp.logical_not(exists))
-        def _(slot=slot):
-            slot[...] = jnp.ones(slot.shape, F32)
-
-    def cells(values, pressure, flagged):
-        total = total_of(values)
-        inverse = 1.0 / total
-        feed = [v * inverse for v in values]
-        moved = flash(feed, jnp.log(pressure), half_vol, half_slope, w_ref)
-        return inverse, total * inverse, [
-            jnp.where(flagged > 0.0, moved[i], feed[i]) for i in range(comps)
-        ]
-
-    blocks = width // TILE
-    chunks = blocks * depth // UNROLL
-
-    def block(step):
-        inner = step // (2 * depth)
-        pair = step % (2 * depth)
-        z = pair // 2
-        place = (1 - inner) * (blocks - 1) * (pair % 2) + inner * (1 + pair % 2)
-        rows = pl.ds(pl.multiple_of(place * TILE, TILE), TILE)
-        values = [comp[i, z, rows, :] for i in range(comps)]
-        inverse, whole, found = cells(values, p[z, rows, :], flags[rows, :])
-        pvi[z, rows, :] = inverse
-        fsum[z, rows, :] = whole
-        for i in range(comps):
-            mob[i, z, rows, :] = found[i]
-        msum[z, rows, :] = total_of(found)
-
-    def chunk(index, carry):
-        def body(step, inner):
-            block(index * UNROLL + step)
-            return inner
-
-        return lax.fori_loop(0, UNROLL, body, carry, unroll=True)
-
-    early = 1 - (here_a // 2) % 2
-    edge_chunks = chunks // 2
-    send_after = early * edge_chunks
-    share_after = edge_chunks + early * (chunks - edge_chunks)
-    lax.fori_loop(0, send_after, chunk, 0)
-    pl.semaphore_wait(barrier, total_of([exists.astype(jnp.int32) for exists in there]))
-    when_there(send.start for send in sends)
+    when_there([send.start for send in sends[2:]], (2, 3))
     lax.fori_loop(send_after, share_after, chunk, 0)
-    for load in loads[8:]:
+    for load in loads[10:]:
         load.wait()
 
     finish(sends, (2, 3))
@@ -397,7 +414,7 @@
         coup[6, z, :, 0:128] = jnp.where(lane == 0, left, right)
         return carry
 
-    lax.fori_loop(0, depth, faces, 0, unroll=2)
+    lax.fori_loop(0, depth, faces, 0, unroll=4)
     stacked = coup[6, :, :, 0:128].reshape(depth * width, 128)
     fysend[...] = jnp.transpose(stacked)[:TILE]
     when_there([share.start for share in shares[2:]], (2, 3))
@@ -459,7 +476,7 @@
         newp[z] = p[z] + gathered * rdiag[z]
         return carry
 
-    lax.fori_loop(0, depth, update, 0, unroll=4)
+    lax.fori_loop(0, depth, update, 0, unroll=8)
 
 
 def write_kernel(value, newp, out_hbm, newp_hbm, sem):
@@ -515,7 +532,7 @@
             scratch((2, YROWS, depth * width)), scratch((2, YROWS, depth * width)),
             scratch((2, 2, depth, span)), scratch((2, 2, depth, span)), scratch((2, depth, span)),
             scratch((TILE, depth * width)), scratch((2, TILE, depth * width)),
-            dma((11,)), dma((4,)), dma((4,)), dma((4,)), dma((4,)),
+            dma((13,)), dma((4,)), dma((4,)), dma((4,)), dma((4,)),
         ],
         compiler_params=pltpu.CompilerParams(
             collective_id=0, has_side_effects=True, vmem_limit_bytes=VMEM_BYTES

time: 25 us -> 23.6 us (0.944)
  Pallas kernels: 24.3 us -> 22.9 us
    pallas_call x1, Pallas kernels: 22.7 us -> 21.3 us  [on_device(): pl.pallas_call(functools.partial(flash_kernel, comps), name='flash', out_...]
where the time goes in v3:
time: 23.6 us; the launch traced here: 23.5 us
  Pallas kernels  22.9 us (97%)
  between operations  0.64 us (3%)
    pallas_call x1, Pallas kernels, on_device(): pl.pallas_call(functools.partial(flash_kernel, comps), name='flash', out_...  21.3 us
    pallas_call x1, Pallas kernels, on_device(): pl.pallas_call(write_kernel, name='write', out_shape=(array(big), array(g...  1.57 us

profile of v3, /device:TPU:6, one launch (start us, length us, event | category | flops | bytes accessed | tf_op | source)
XLA Modules:
  0.0 23.5 jit_solution(866955371027226663)
XLA Ops:
  0.6 21.3 %flash.1 = (f32[9,8,32,256]{3,2,1,0:T(8,128)S(1)}, f32[8,32,256]{2,1,0:T(8,128)S(1)}) custom-call(f32[8,32,256]{2,1,0:T(8,128)} %p_hbm.1, f32[9,8,32,256]{3,2,1,0:T(8,128)} %comp_hbm.1, f32[9,8,32,256]{3,2,1,0:T(8,128)} %mass_hbm.1, f32[8,32,256]{2,1,0:T(8,128)} %pv_hbm.1, f32[8,32,256]{2,1,0:T(8,128)} %tx_hbm.1, f32[8,32,256]{2,1,0:T(8,128)} %ty_hbm.1, ...), custom_call_target="tpu_custom_call" | custom-call | tf_op jit(solution)/shard_map/flash/pallas_call | solution.py:513
  21.9 1.6 %write.1 = (f32[9,8,32,256]{3,2,1,0:T(8,128)}, f32[8,32,256]{2,1,0:T(8,128)}) custom-call(f32[9,8,32,256]{3,2,1,0:T(8,128)S(1)} %get-tuple-element.4.value, f32[8,32,256]{2,1,0:T(8,128)S(1)} %get-tuple-element.5.newp), custom_call_target="tpu_custom_call" | custom-call | tf_op jit(solution)/shard_map/write/pallas_call | solution.py:549

commit v4 on v3

--- a/solution.py
+++ b/solution.py
@@ -45,13 +45,11 @@
 
 
 def mixed(w_ref, parts):
-    stack = jnp.concatenate(parts, axis=0)
+    stack = jnp.concatenate(parts + [jnp.zeros_like(parts[0])], axis=0)
     high = stack.astype(BF16)
     low = (stack - high.astype(F32)).astype(BF16)
-    out = (
-        jnp.dot(w_ref[0], high, preferred_element_type=F32)
-        + jnp.dot(w_ref[1], high, preferred_element_type=F32)
-        + jnp.dot(w_ref[0], low, preferred_element_type=F32)
+    out = jnp.dot(
+        w_ref[...], jnp.concatenate([high, low, high], axis=0), preferred_element_type=F32
     )
     return [out[i * TILE : (i + 1) * TILE] for i in range(len(parts))]
 
@@ -178,7 +176,11 @@
     pl.when(early == 0)(send_x)
     for load in loads[5:8]:
         load.wait()
-    w_ref[0], w_ref[1] = split_matrix(mix[...], comps)
+    high_part, low_part = split_matrix(mix[...], comps)
+    blank = jnp.zeros((comps * TILE, TILE), BF16)
+    w_ref[...] = jnp.concatenate(
+        [high_part, blank, high_part, blank, low_part, blank], axis=1
+    )
     half_vol = [(0.5 if i < light_count else -0.5) * vol[i] for i in range(comps)]
     half_slope = [0.5 * slope[i] for i in range(comps)]
     for exists, slot in zip(there, (xrecv.at[0], xrecv.at[1], yrecv.at[0], yrecv.at[1])):
@@ -520,7 +522,7 @@
             scratch(big), scratch(big), scratch(big), scratch(grid), scratch((7,) + grid),
             scratch((2, comps, depth, span)), scratch((depth * width, 128)),
             scratch(grid), scratch(grid), scratch(grid), scratch(grid), scratch(grid),
-            pltpu.VMEM((2, comps * TILE, comps * TILE), BF16),
+            pltpu.VMEM((comps * TILE, 3 * (comps + 1) * TILE), BF16),
             scratch((comps, comps)),
             pltpu.SMEM((comps,), F32), pltpu.SMEM((comps,), F32),
             pltpu.SMEM(two_phase.shape, jnp.int32),

time: 23.6 us -> 23.5 us (level)
  no operation moved by 1% of the time
where the time goes in v4:
time: 23.5 us; the launch traced here: 23.4 us
  Pallas kernels  22.8 us (97%)
  between operations  0.64 us (3%)
    pallas_call x1, Pallas kernels, on_device(): pl.pallas_call(functools.partial(flash_kernel, comps), name='flash', out_...  21.2 us
    pallas_call x1, Pallas kernels, on_device(): pl.pallas_call(write_kernel, name='write', out_shape=(array(big), array(g...  1.57 us

profile of v4, /device:TPU:6, one launch (start us, length us, event | category | flops | bytes accessed | tf_op | source)
XLA Modules:
  0.0 23.4 jit_solution(13700191845358286158)
XLA Ops:
  0.6 21.2 %flash.1 = (f32[9,8,32,256]{3,2,1,0:T(8,128)S(1)}, f32[8,32,256]{2,1,0:T(8,128)S(1)}) custom-call(f32[8,32,256]{2,1,0:T(8,128)} %p_hbm.1, f32[9,8,32,256]{3,2,1,0:T(8,128)} %comp_hbm.1, f32[9,8,32,256]{3,2,1,0:T(8,128)} %mass_hbm.1, f32[8,32,256]{2,1,0:T(8,128)} %pv_hbm.1, f32[8,32,256]{2,1,0:T(8,128)} %tx_hbm.1, f32[8,32,256]{2,1,0:T(8,128)} %ty_hbm.1, ...), custom_call_target="tpu_custom_call" | custom-call | tf_op jit(solution)/shard_map/flash/pallas_call | solution.py:515
  21.9 1.6 %write.1 = (f32[9,8,32,256]{3,2,1,0:T(8,128)}, f32[8,32,256]{2,1,0:T(8,128)}) custom-call(f32[9,8,32,256]{3,2,1,0:T(8,128)S(1)} %get-tuple-element.4.value, f32[8,32,256]{2,1,0:T(8,128)S(1)} %get-tuple-element.5.newp), custom_call_target="tpu_custom_call" | custom-call | tf_op jit(solution)/shard_map/write/pallas_call | solution.py:551

commit v5 on v4

--- a/solution.py
+++ b/solution.py
@@ -223,12 +223,15 @@
         return lax.fori_loop(0, UNROLL, body, carry, unroll=True)
 
     edge_chunks = chunks // 2
-    send_after = early * edge_chunks
+    far = (here_a % 16 == 0).astype(jnp.int32)
+    most = (here_l == 0).astype(jnp.int32)
+    some = (here_l < 3).astype(jnp.int32)
+    send_after = early * (edge_chunks + most + (1 - most) * some * far)
     share_after = edge_chunks + early * (chunks - edge_chunks)
+    for load in loads[8:10]:
+        load.wait()
     lax.fori_loop(0, send_after, chunk, 0)
     pl.when(early == 1)(send_x)
-    for load in loads[8:10]:
-        load.wait()
 
     def pack_y(z, carry):
         packed = jnp.zeros((width, 128), F32)

time: 23.5 us -> 23.5 us (level)
  no operation moved by 1% of the time
where the time goes in v5:
time: 23.5 us; the launch traced here: 23.4 us
  Pallas kernels  22.8 us (97%)
  between operations  0.64 us (3%)
    pallas_call x1, Pallas kernels, on_device(): pl.pallas_call(functools.partial(flash_kernel, comps), name='flash', out_...  21.2 us
    pallas_call x1, Pallas kernels, on_device(): pl.pallas_call(write_kernel, name='write', out_shape=(array(big), array(g...  1.57 us

profile of v5, /device:TPU:6, one launch (start us, length us, event | category | flops | bytes accessed | tf_op | source)
XLA Modules:
  0.0 23.4 jit_solution(1678729452784275783)
XLA Ops:
  0.6 21.2 %flash.1 = (f32[9,8,32,256]{3,2,1,0:T(8,128)S(1)}, f32[8,32,256]{2,1,0:T(8,128)S(1)}) custom-call(f32[8,32,256]{2,1,0:T(8,128)} %p_hbm.1, f32[9,8,32,256]{3,2,1,0:T(8,128)} %comp_hbm.1, f32[9,8,32,256]{3,2,1,0:T(8,128)} %mass_hbm.1, f32[8,32,256]{2,1,0:T(8,128)} %pv_hbm.1, f32[8,32,256]{2,1,0:T(8,128)} %tx_hbm.1, f32[8,32,256]{2,1,0:T(8,128)} %ty_hbm.1, ...), custom_call_target="tpu_custom_call" | custom-call | tf_op jit(solution)/shard_map/flash/pallas_call | solution.py:518
  21.9 1.6 %write.1 = (f32[9,8,32,256]{3,2,1,0:T(8,128)}, f32[8,32,256]{2,1,0:T(8,128)}) custom-call(f32[9,8,32,256]{3,2,1,0:T(8,128)S(1)} %get-tuple-element.4.value, f32[8,32,256]{2,1,0:T(8,128)S(1)} %get-tuple-element.5.newp), custom_call_target="tpu_custom_call" | custom-call | tf_op jit(solution)/shard_map/write/pallas_call | solution.py:554
